TPU v7x, 32 devices: a whole 2x2x4 slice. The times are simulated.
32 devices in a mesh: rows: 32 (over z, y, x, core).
Axes of the slice: x: 2, y: 2, z: 4, core: 2. Of those that a mesh axis runs over, the one named last changes fastest.
Arguments:
- snapshots: float32 [262144, 128], P('rows')
- send_list: int32 [1024, 64], P('rows'), may hold values from 0 to 8191
- stencil: int32 [524288, 8], P('rows'), may hold values from 0 to 2047, as said below
- weights: float32 [524288, 8], P('rows'), may hold values from 0.2 to 1
Outputs:
- basis: float32 [524288, 128], P('rows')
- r_factor: float32 [128, 128], replicated
Inputs may be any that keep to these rules, and one draw needn't show every extreme that they name: `send_list`: every slot carries a node; a node may fill several slots. `stencil`: all 8 donors of a row lie on one peer: local row k of device d takes them from peer (d + k // 512) mod 32. Every slot that a device receives is read by some of its rows.
All inputs are finite; a program needn't handle non-finite values.
Results may differ from a plain program's by a relative error of at most 0.0003.
Values sent between devices are 32-bit elements; how exact they have to be, the bound alone decides.
No kernel may reach another device: no remote copies, remote signals or barrier semaphores. Data moves between devices by JAX's collectives and lax.ppermute only.
A program may use at most 192 MiB of HBM per device.

v0:
```python
import jax
import jax.numpy as jnp
from jax import lax
from jax.sharding import PartitionSpec as P


def product(left, right):
    return jnp.dot(left, right, precision=lax.Precision.HIGHEST, preferred_element_type=jnp.float32)


def upper_inverse(upper):
    count = upper.shape[0]
    if count == 1:
        return 1.0 / upper
    half = count // 2
    top_inv = upper_inverse(upper[:half, :half])
    low_inv = upper_inverse(upper[half:, half:])
    corner = -product(product(top_inv, upper[:half, half:]), low_inv)
    zeros_block = jnp.zeros((count - half, half), jnp.float32)
    top_rows = jnp.concatenate([top_inv, corner], axis=1)
    low_rows = jnp.concatenate([zeros_block, low_inv], axis=1)
    return jnp.concatenate([top_rows, low_rows], axis=0)


def normed_factor(block, total_rows):
    local = product(block.T, block)
    gram = lax.psum(local, "rows")
    upper = jnp.linalg.cholesky(gram / total_rows).T
    return upper


def body(snapshots, send_list, stencil, weights):
    peers = lax.axis_size("rows")
    row_count = stencil.shape[0]
    total_rows = row_count * peers
    outgoing = snapshots[send_list]
    received = lax.all_to_all(outgoing, "rows", split_axis=0, concat_axis=0, tiled=True)
    flat = received.reshape(received.shape[0] * received.shape[1], received.shape[2])
    field = jnp.zeros((row_count, flat.shape[1]), jnp.float32)
    for s in range(stencil.shape[1]):
        field = field + weights[:, s][:, None] * flat[stencil[:, s]]
    first = normed_factor(field, total_rows)
    middle = product(field, upper_inverse(first))
    second = normed_factor(middle, total_rows)
    basis = product(middle, upper_inverse(second))
    r_factor = product(second, first)
    return (basis, r_factor)


def solution(mesh):
    return jax.shard_map(
        body,
        mesh=mesh,
        in_specs=(P("rows", None), P("rows", None), P("rows", None), P("rows", None)),
        out_specs=(P("rows", None), P()),
        check_vma=False,
    )
```

profile of v0, /device:TPU:1, one launch (start us, length us, event | category | flops | bytes accessed | tf_op | source)
XLA Modules:
  0.0 1185.2 jit_solution(2221506955138115921)
XLA Ops:
  7.2 0.8 compare_select_fusion.8
  8.1 9.8 gather_fusion
  17.9 7.1 all-to-all-start
  25.1 0.7 compare_select_fusion.7
  25.9 1.1 fusion.1773
  27.0 23.3 %all-to-all-done = f32[32,64,128]{2,1,0:T(8,128)S(1)} async-done(((f32[32,64,128]{2,1,0:T(8,128)}), f32[32,64,128]{2,1,0:T(8,128)S(1)}, u32[]{:S(2)}, u32[]{:S(2)}) %all-to-all-start) | async-done | bytes 1048608 | tf_op jit(solution)/shard_map/all_to_all | solution.py:37
  50.3 54.7 %gather_fusion.1 = f32[16384,128]{1,0:T(8,128)} fusion(f32[2048,128]{1,0:T(8,128)S(1)} %bitcast.288, s32[16384]{0:T(1024)S(1)} %broadcast_clamp_fusion.7), kind=kCustom, calls=%fused_computation.1 | custom fusion | bytes 16842752 | tf_op jit(solution)/shard_map/gather | solution.py:41
  105.1 54.8 %gather_fusion.2 = f32[16384,128]{1,0:T(8,128)} fusion(f32[2048,128]{1,0:T(8,128)S(1)} %bitcast.289, s32[16384]{0:T(1024)S(1)} %broadcast_clamp_fusion.6), kind=kCustom, calls=%fused_computation.2 | custom fusion | bytes 16842752 | tf_op jit(solution)/shard_map/gather | solution.py:41
  159.9 54.8 %gather_fusion.3 = f32[16384,128]{1,0:T(8,128)} fusion(f32[2048,128]{1,0:T(8,128)S(1)} %bitcast.290, s32[16384]{0:T(1024)S(1)} %broadcast_clamp_fusion.5), kind=kCustom, calls=%fused_computation.3 | custom fusion | bytes 16842752 | tf_op jit(solution)/shard_map/gather | solution.py:41
  214.6 54.8 %gather_fusion.4 = f32[16384,128]{1,0:T(8,128)} fusion(f32[2048,128]{1,0:T(8,128)S(1)} %bitcast.291, s32[16384]{0:T(1024)S(1)} %broadcast_clamp_fusion.4), kind=kCustom, calls=%fused_computation.4 | custom fusion | bytes 16842752 | tf_op jit(solution)/shard_map/gather | solution.py:41
  269.4 54.8 %gather_fusion.5 = f32[16384,128]{1,0:T(8,128)} fusion(f32[2048,128]{1,0:T(8,128)S(1)} %bitcast.292, s32[16384]{0:T(1024)S(1)} %broadcast_clamp_fusion.3), kind=kCustom, calls=%fused_computation.5 | custom fusion | bytes 16842752 | tf_op jit(solution)/shard_map/gather | solution.py:41
  324.2 54.8 %gather_fusion.6 = f32[16384,128]{1,0:T(8,128)} fusion(f32[2048,128]{1,0:T(8,128)S(1)} %bitcast.293, s32[16384]{0:T(1024)S(1)} %broadcast_clamp_fusion.2), kind=kCustom, calls=%fused_computation.6 | custom fusion | bytes 16842752 | tf_op jit(solution)/shard_map/gather | solution.py:41
  379.0 54.7 %gather_fusion.7 = f32[16384,128]{1,0:T(8,128)} fusion(f32[2048,128]{1,0:T(8,128)S(1)} %bitcast.294, s32[16384]{0:T(1024)S(1)} %broadcast_clamp_fusion.1), kind=kCustom, calls=%fused_computation.7 | custom fusion | bytes 16842752 | tf_op jit(solution)/shard_map/gather | solution.py:41
  433.8 54.9 %gather_fusion.8 = f32[16384,128]{1,0:T(8,128)} fusion(f32[2048,128]{1,0:T(8,128)S(1)} %bitcast.295, s32[16384]{0:T(1024)S(1)} %broadcast_clamp_fusion), kind=kCustom, calls=%fused_computation.8 | custom fusion | bytes 16842752 | tf_op jit(solution)/shard_map/gather | solution.py:41
  488.7 25.8 %multiply_add_fusion = f32[16384,128]{1,0:T(8,128)S(1)} fusion(f32[16384,128]{1,0:T(8,128)} %gather_fusion.8, f32[16384,128]{1,0:T(8,128)} %gather_fusion.7, f32[16384,128]{1,0:T(8,128)} %gather_fusion.6, f32[16384,128]{1,0:T(8,128)} %gather_fusion.5, f32[16384,128]{1,0:T(8,128)} %gather_fusion.4, f32[16384,128]{1,0:T(8,128)} %gather_fusion.3, ...), kind=kLoop, calls=%fused_computation.9 | loop fusion | flops 31457280 | bytes 76021760 | tf_op jit(solution)/shard_map/add | solution.py:41
  514.5 3.4 copy-done.1
  517.9 14.9 %fusion.1794 = f32[128,128]{0,1:T(8,128)} fusion(f32[16384,128]{1,0:T(8,128)S(1)} %multiply_add_fusion), kind=kOutput, calls=%fused_computation.2092 | convolution fusion | flops 3221225472 | bytes 8454144 | tf_op jit(solution)/shard_map/dot_general | solution.py:8
  532.8 118.9 %all-reduce.129.cloned.1.call-done = f32[128,128]{0,1:T(8,128)} async-done(((f32[128,128]{0,1:T(8,128)}), f32[128,128]{0,1:T(8,128)}) %all-reduce.129.cloned.1.call-update) | async-done | bytes 65552 | tf_op jit(solution)/shard_map/psum | solution.py:27
  651.7 0.8 broadcast_multiply_fusion.1
  652.7 0.9 fusion.65
  653.5 11.7 cholesky.44
  665.3 0.6 compare_reduce_fusion.1
  665.9 0.6 fusion.67
  666.5 0.7 fusion.1785
  667.2 0.7 fusion.1784
  667.9 0.7 fusion.1786
  668.6 0.7 fusion.1787
  669.4 0.7 fusion.1788
  670.1 0.6 slice.3140
  670.7 0.7 fusion.1790
  671.4 0.7 fusion.1789
  672.1 0.7 fusion.1791
  672.9 0.7 fusion.1792
  673.6 0.7 fusion.1793
  674.3 0.7 slice.3268
  712.8 0.3 fusion.520
  751.4 0.3 fusion.544
  829.0 0.3 fusion.592
  830.6 0.3 fusion.80
  831.1 10.1 fusion.13
  841.2 3.3 copy-done
  844.5 14.6 %fusion.1795 = f32[128,128]{0,1:T(8,128)} fusion(f32[16384,128]{1,0:T(8,128)S(1)} %fusion.13), kind=kOutput, calls=%fused_computation.2093 | convolution fusion | flops 3221225472 | bytes 8454144 | tf_op jit(solution)/shard_map/dot_general | solution.py:8
  859.1 118.5 %all-reduce.131.cloned.1.call-done = f32[128,128]{0,1:T(8,128)} async-done(((f32[128,128]{0,1:T(8,128)}), f32[128,128]{0,1:T(8,128)}) %all-reduce.131.cloned.1.call-update) | async-done | bytes 65552 | tf_op jit(solution)/shard_map/psum | solution.py:27
  977.6 0.8 broadcast_multiply_fusion
  978.5 0.9 fusion.64
  979.4 11.7 cholesky.55
  991.2 0.6 compare_reduce_fusion
  991.8 2.1 fusion.66
  993.9 0.7 fusion.68
  994.6 0.7 fusion.1775
  995.3 0.7 fusion.1774
  996.0 0.7 fusion.1776
  996.8 0.7 fusion.1778
  997.5 0.7 fusion.1777
  998.2 0.6 slice.3395
  998.8 0.7 fusion.1780
  999.6 0.7 fusion.1779
  1000.3 0.7 fusion.1781
  1001.0 0.7 fusion.1783
  1001.8 0.7 fusion.1782
  1002.5 0.7 slice.3523
  1129.3 0.4 convolution_negate_fusion.33
  1160.2 0.3 fusion.104
  1160.7 17.2 %fusion.28 = f32[16384,128]{1,0:T(8,128)} fusion(f32[16384,128]{1,0:T(8,128)} %copy-done, f32[1,1]{0,1:T(1,128)} %constant.46.clone.1, f32[64,64]{0,1:T(8,128)S(1)} %fusion.116, f32[64,64]{0,1:T(8,128)S(1)} %convolution_negate_fusion, f32[32,64]{0,1:T(8,128)S(1)} %concatenate.2854, f32[32,32]{0,1:T(8,128)S(1)} %convolution_negate_fusion.3, ...), kind=kOutput, calls=%fused_computation.185 | convolution fusion | flops 3221504000 | bytes 16826368 | tf_op jit(solution)/shard_map/dot_general | solution.py:8
  (462 shorter events, 60.5 us)
Async XLA Ops:
  7.2 17.9 %copy-start.2 = (s32[16384,8]{0,1:T(8,128)S(1)}, s32[16384,8]{0,1:T(8,128)}, u32[]{:S(2)}) copy-start(s32[16384,8]{0,1:T(8,128)} %param.7) | copy-start | bytes 1572868
  7.2 18.7 %copy-start.3 = (f32[16384,8]{0,1:T(8,128)S(1)}, f32[16384,8]{0,1:T(8,128)}, u32[]{:S(2)}) copy-start(f32[16384,8]{0,1:T(8,128)} %param.8) | copy-start | bytes 1572868
  17.9 32.4 %all-to-all-start = ((f32[32,64,128]{2,1,0:T(8,128)}), f32[32,64,128]{2,1,0:T(8,128)S(1)}, u32[]{:S(2)}, u32[]{:S(2)}) async-start(f32[32,64,128]{2,1,0:T(8,128)} %bitcast.1), calls=%async_computation | async-start | bytes 2097152 | tf_op jit(solution)/shard_map/all_to_all | solution.py:37
  25.0 626.7 %all-reduce.129.cloned.1.call-start = ((), (), s32[]{:S(2)}) async-start(), calls=%async_computation.1 | async-start | bytes 131072 | tf_op jit(solution)/shard_map/psum | solution.py:27
  433.7 54.9 %copy-start.4 = (f32[16384,1]{0,1:T(1,128)S(1)}, f32[16384,1]{0,1:T(1,128)}, u32[]{:S(2)}) copy-start(f32[16384,1]{0,1:T(1,128)} %get-tuple-element.3) | copy-start | bytes 196612
  433.7 54.9 %copy-start.5 = (f32[16384,1]{0,1:T(1,128)S(1)}, f32[16384,1]{0,1:T(1,128)}, u32[]{:S(2)}) copy-start(f32[16384,1]{0,1:T(1,128)} %get-tuple-element.4) | copy-start | bytes 196612
  433.7 54.9 %copy-start.6 = (f32[16384,1]{0,1:T(1,128)S(1)}, f32[16384,1]{0,1:T(1,128)}, u32[]{:S(2)}) copy-start(f32[16384,1]{0,1:T(1,128)} %get-tuple-element.5) | copy-start | bytes 196612
  433.7 54.9 %copy-start.7 = (f32[16384,1]{0,1:T(1,128)S(1)}, f32[16384,1]{0,1:T(1,128)}, u32[]{:S(2)}) copy-start(f32[16384,1]{0,1:T(1,128)} %get-tuple-element.6) | copy-start | bytes 196612
  433.8 54.9 %copy-start.8 = (f32[16384,1]{0,1:T(1,128)S(1)}, f32[16384,1]{0,1:T(1,128)}, u32[]{:S(2)}) copy-start(f32[16384,1]{0,1:T(1,128)} %get-tuple-element.7) | copy-start | bytes 196612
  433.8 54.9 %copy-start.9 = (f32[16384,1]{0,1:T(1,128)S(1)}, f32[16384,1]{0,1:T(1,128)}, u32[]{:S(2)}) copy-start(f32[16384,1]{0,1:T(1,128)} %get-tuple-element.8) | copy-start | bytes 196612
  433.8 54.9 %copy-start.10 = (f32[16384,1]{0,1:T(1,128)S(1)}, f32[16384,1]{0,1:T(1,128)}, u32[]{:S(2)}) copy-start(f32[16384,1]{0,1:T(1,128)} %get-tuple-element.9) | copy-start | bytes 196612
  433.8 54.9 %copy-start.11 = (f32[16384,1]{0,1:T(1,128)S(1)}, f32[16384,1]{0,1:T(1,128)}, u32[]{:S(2)}) copy-start(f32[16384,1]{0,1:T(1,128)} %get-tuple-element.10) | copy-start | bytes 196612
  514.5 3.4 copy-start.1
  532.8 444.8 %all-reduce.131.cloned.1.call-start = ((), (), s32[]{:S(2)}) async-start(), calls=%async_computation.2 | async-start | bytes 131072 | tf_op jit(solution)/shard_map/psum | solution.py:27
  841.2 3.3 copy-start
Sparse Core Ops, SparseCore 0:
  532.9 118.7 all-reduce.128
  859.2 118.3 all-reduce.130
where the time goes:
time: 1190 us
  local copies, waits for them, and re-layouts  474 us (40%)
  between operations  267 us (22%)
  waiting for transfers between devices  261 us (22%)
  matrix products  111 us (9%)
  other arithmetic  66.1 us (6%)
    gather x8, local copies, waits for them, and re-layouts, body(): field = field + weights[:, s][:, None] * flat[stencil[:, s]]  438 us
    psum x2, waiting for transfers between devices, normed_factor(): gram = lax.psum(local, 'rows')  237 us
    dot_general x257, matrix products, product(): jnp.dot(left, right, precision=lax.Precision.HIGHEST, preferred_element_t...  111 us
    add x1, other arithmetic, body(): field = field + weights[:, s][:, None] * flat[stencil[:, s]]  25.8 us
    another operation x6, other arithmetic, normed_factor(): upper = jnp.linalg.cholesky(gram / total_rows).T  24.8 us
  transfers between devices with their start and end apart: 3, of which 3 were waited for; matrix products, arithmetic and copies ran while one was open for 0% of the time, Pallas kernels for 0%

commit v1 on v0

--- a/solution.py
+++ b/solution.py
@@ -24,7 +24,9 @@
 
 def normed_factor(block, total_rows):
     local = product(block.T, block)
-    gram = lax.psum(local, "rows")
+    gram = local
+    for hop in (1, 2, 4, 8, 16):
+        gram = gram + lax.ppermute(gram, "rows", [(dev, dev ^ hop) for dev in range(32)])
     upper = jnp.linalg.cholesky(gram / total_rows).T
     return upper
 

time: 1190 us -> 972 us (0.82)
  waiting for transfers between devices: 261 us -> 46.3 us
  between operations: 267 us -> 253 us
  starting transfers between devices: 7.18 us -> 20.9 us
    psum x2 -> x0, waiting for transfers between devices: 237 us -> none  [normed_factor(): gram = lax.psum(local, 'rows')]
    ppermute x0 -> x10, waiting for transfers between devices: none -> 22.9 us  [normed_factor(): lax.ppermute(gram, 'rows', [(dev, dev ^ hop) for dev in range(32)])]
    ppermute x0 -> x10, starting transfers between devices: none -> 13.8 us  [normed_factor(): lax.ppermute(gram, 'rows', [(dev, dev ^ hop) for dev in range(32)])]
  transfers between devices with their start and end apart: 3 -> 11, of which waited for: 3 -> 11; matrix products, arithmetic and copies ran while one was open for 0% -> 0% of each run, Pallas kernels for 0% -> 0%
where the time goes in v1:
time: 972 us; the launch traced here: 960 us
  local copies, waits for them, and re-layouts  467 us (48%)
  between operations  253 us (26%)
  matrix products  110 us (11%)
  other arithmetic  63.1 us (6%)
  waiting for transfers between devices  46.3 us (5%)
  starting transfers between devices  20.9 us (2%)
    gather x8, local copies, waits for them, and re-layouts, body(): field = field + weights[:, s][:, None] * flat[stencil[:, s]]  438 us
    dot_general x257, matrix products, product(): jnp.dot(left, right, precision=lax.Precision.HIGHEST, preferred_element_t...  110 us
    add x1, other arithmetic, body(): field = field + weights[:, s][:, None] * flat[stencil[:, s]]  25.9 us
    another operation x6, other arithmetic, normed_factor(): upper = jnp.linalg.cholesky(gram / total_rows).T  24.8 us
    all_to_all x1, waiting for transfers between devices, body(): lax.all_to_all(outgoing, 'rows', split_axis=0, concat_axis=0, tiled=True)  23.4 us
    ppermute x10, waiting for transfers between devices, normed_factor(): lax.ppermute(gram, 'rows', [(dev, dev ^ hop) for dev in range(32)])  22.9 us
  transfers between devices with their start and end apart: 11, of which 11 were waited for; matrix products, arithmetic and copies ran while one was open for 0% of the time, Pallas kernels for 0%

profile of v1, /device:TPU:1, one launch (start us, length us, event | category | flops | bytes accessed | tf_op | source)
XLA Modules:
  0.0 960.2 jit_solution(1155112433441242662)
XLA Ops:
  0.7 0.8 compare_select_fusion.8
  1.5 9.8 %gather_fusion = f32[2048,128]{1,0:T(8,128)} fusion(f32[8192,128]{1,0:T(8,128)} %param.5, s32[2048]{0:T(1024)S(1)} %broadcast_clamp_fusion.8), kind=kCustom, calls=%fused_computation | custom fusion | bytes 2105344 | tf_op jit(solution)/shard_map/gather | solution.py:38
  11.4 7.1 all-to-all-start
  18.5 0.7 compare_select_fusion.7
  19.3 1.1 fusion.1773
  20.4 23.4 %all-to-all-done = f32[32,64,128]{2,1,0:T(8,128)S(1)} async-done(((f32[32,64,128]{2,1,0:T(8,128)}), f32[32,64,128]{2,1,0:T(8,128)S(1)}, u32[]{:S(2)}, u32[]{:S(2)}) %all-to-all-start) | async-done | bytes 1048608 | tf_op jit(solution)/shard_map/all_to_all | solution.py:39
  43.8 54.8 %gather_fusion.1 = f32[16384,128]{1,0:T(8,128)} fusion(f32[2048,128]{1,0:T(8,128)S(1)} %bitcast.288, s32[16384]{0:T(1024)S(1)} %broadcast_clamp_fusion.7), kind=kCustom, calls=%fused_computation.1 | custom fusion | bytes 16842752 | tf_op jit(solution)/shard_map/gather | solution.py:43
  98.6 54.8 %gather_fusion.2 = f32[16384,128]{1,0:T(8,128)} fusion(f32[2048,128]{1,0:T(8,128)S(1)} %bitcast.289, s32[16384]{0:T(1024)S(1)} %broadcast_clamp_fusion.6), kind=kCustom, calls=%fused_computation.2 | custom fusion | bytes 16842752 | tf_op jit(solution)/shard_map/gather | solution.py:43
  153.3 54.8 %gather_fusion.3 = f32[16384,128]{1,0:T(8,128)} fusion(f32[2048,128]{1,0:T(8,128)S(1)} %bitcast.290, s32[16384]{0:T(1024)S(1)} %broadcast_clamp_fusion.5), kind=kCustom, calls=%fused_computation.3 | custom fusion | bytes 16842752 | tf_op jit(solution)/shard_map/gather | solution.py:43
  208.1 54.8 %gather_fusion.4 = f32[16384,128]{1,0:T(8,128)} fusion(f32[2048,128]{1,0:T(8,128)S(1)} %bitcast.291, s32[16384]{0:T(1024)S(1)} %broadcast_clamp_fusion.4), kind=kCustom, calls=%fused_computation.4 | custom fusion | bytes 16842752 | tf_op jit(solution)/shard_map/gather | solution.py:43
  262.9 54.7 %gather_fusion.5 = f32[16384,128]{1,0:T(8,128)} fusion(f32[2048,128]{1,0:T(8,128)S(1)} %bitcast.292, s32[16384]{0:T(1024)S(1)} %broadcast_clamp_fusion.3), kind=kCustom, calls=%fused_computation.5 | custom fusion | bytes 16842752 | tf_op jit(solution)/shard_map/gather | solution.py:43
  317.6 54.9 %gather_fusion.6 = f32[16384,128]{1,0:T(8,128)} fusion(f32[2048,128]{1,0:T(8,128)S(1)} %bitcast.293, s32[16384]{0:T(1024)S(1)} %broadcast_clamp_fusion.2), kind=kCustom, calls=%fused_computation.6 | custom fusion | bytes 16842752 | tf_op jit(solution)/shard_map/gather | solution.py:43
  372.5 54.8 %gather_fusion.7 = f32[16384,128]{1,0:T(8,128)} fusion(f32[2048,128]{1,0:T(8,128)S(1)} %bitcast.294, s32[16384]{0:T(1024)S(1)} %broadcast_clamp_fusion.1), kind=kCustom, calls=%fused_computation.7 | custom fusion | bytes 16842752 | tf_op jit(solution)/shard_map/gather | solution.py:43
  427.3 54.9 %gather_fusion.8 = f32[16384,128]{1,0:T(8,128)} fusion(f32[2048,128]{1,0:T(8,128)S(1)} %bitcast.295, s32[16384]{0:T(1024)S(1)} %broadcast_clamp_fusion), kind=kCustom, calls=%fused_computation.8 | custom fusion | bytes 16842752 | tf_op jit(solution)/shard_map/gather | solution.py:43
  482.2 25.9 %multiply_add_fusion = f32[16384,128]{1,0:T(8,128)S(1)} fusion(f32[16384,128]{1,0:T(8,128)} %gather_fusion.8, f32[16384,128]{1,0:T(8,128)} %gather_fusion.7, f32[16384,128]{1,0:T(8,128)} %gather_fusion.6, f32[16384,128]{1,0:T(8,128)} %gather_fusion.5, f32[16384,128]{1,0:T(8,128)} %gather_fusion.4, f32[16384,128]{1,0:T(8,128)} %gather_fusion.3, ...), kind=kLoop, calls=%fused_computation.9 | loop fusion | flops 31457280 | bytes 76021760 | tf_op jit(solution)/shard_map/add | solution.py:43
  508.1 14.4 %fusion.1794 = f32[128,128]{0,1:T(8,128)S(1)} fusion(f32[16384,128]{1,0:T(8,128)S(1)} %multiply_add_fusion), kind=kOutput, calls=%fused_computation.2092 | convolution fusion | flops 3221225472 | bytes 8454144 | tf_op jit(solution)/shard_map/dot_general | solution.py:8
  522.5 1.2 collective-permute-start
  523.7 0.9 collective-permute-done
  524.6 1.2 collective-permute-start.1
  525.9 1.9 collective-permute-done.1
  527.8 1.3 collective-permute-start.2
  529.1 1.9 collective-permute-done.2
  531.6 2.6 collective-permute-done.3
  534.2 1.6 collective-permute-start.4
  535.8 3.2 collective-permute-done.4
  539.1 11.7 %cholesky.44 = f32[128,128]{1,0:T(8,128)S(1)} custom-call(f32[128,128]{1,0:T(8,128)S(1)} %fusion.65), custom_call_target="Cholesky" | custom-call | tf_op jit(solution)/shard_map/jit(cholesky)/cholesky | solution.py:30
  550.9 0.7 compare_reduce_fusion.1
  551.5 0.6 fusion.67
  552.1 0.7 fusion.1785
  552.9 0.7 fusion.1784
  553.6 0.7 fusion.1786
  554.3 0.7 fusion.1787
  555.1 0.7 fusion.1788
  556.3 0.7 fusion.1790
  557.1 0.7 fusion.1789
  557.8 0.7 fusion.1791
  558.5 0.7 fusion.1792
  559.2 0.7 fusion.1793
  716.7 9.9 %fusion.13 = f32[16384,128]{1,0:T(8,128)S(1)} fusion(f32[16384,128]{1,0:T(8,128)} %copy-done.1, f32[1,1]{0,1:T(1,128)} %constant.46.clone.1, f32[64,64]{0,1:T(8,128)S(1)} %fusion.92, f32[64,64]{0,1:T(8,128)S(1)} %convolution_negate_fusion.1, f32[32,64]{0,1:T(8,128)S(1)} %concatenate.2473, f32[32,32]{0,1:T(8,128)S(1)} %convolution_negate_fusion.5, ...), kind=kOutput, calls=%fused_computation.171 | convolution fusion | flops 3221504000 | bytes 16826368 | tf_op jit(solution)/shard_map/dot_general | solution.py:8
  726.6 14.2 %fusion.1795 = f32[128,128]{0,1:T(8,128)S(1)} fusion(f32[16384,128]{1,0:T(8,128)S(1)} %fusion.13), kind=kOutput, calls=%fused_computation.2093 | convolution fusion | flops 3221225472 | bytes 8454144 | tf_op jit(solution)/shard_map/dot_general | solution.py:8
  740.8 5.0 collective-permute-start.5
  745.8 0.9 collective-permute-done.5
  747.3 2.6 collective-permute-done.6
  749.9 1.3 collective-permute-start.7
  751.2 1.9 collective-permute-done.7
  753.6 2.7 collective-permute-done.8
  756.9 4.2 collective-permute-done.9
  761.2 11.7 %cholesky.55 = f32[128,128]{1,0:T(8,128)S(1)} custom-call(f32[128,128]{1,0:T(8,128)S(1)} %fusion.64), custom_call_target="Cholesky" | custom-call | tf_op jit(solution)/shard_map/jit(cholesky)/cholesky | solution.py:30
  773.0 0.6 compare_reduce_fusion
  773.6 2.2 fusion.66
  775.8 0.7 fusion.68
  776.5 0.7 fusion.1775
  777.2 0.7 fusion.1774
  777.9 0.7 fusion.1776
  778.7 0.7 fusion.1778
  779.4 0.7 fusion.1777
  780.1 0.6 slice.3395
  780.8 0.7 fusion.1780
  781.5 0.7 fusion.1779
  782.2 0.7 fusion.1781
  783.0 0.7 fusion.1783
  783.7 0.7 fusion.1782
  784.4 0.7 slice.3523
  942.8 17.2 %fusion.28 = f32[16384,128]{1,0:T(8,128)} fusion(f32[16384,128]{1,0:T(8,128)} %copy-done, f32[1,1]{0,1:T(1,128)} %constant.46.clone.1, f32[64,64]{0,1:T(8,128)S(1)} %fusion.116, f32[64,64]{0,1:T(8,128)S(1)} %convolution_negate_fusion, f32[32,64]{0,1:T(8,128)S(1)} %concatenate.2854, f32[32,32]{0,1:T(8,128)S(1)} %convolution_negate_fusion.3, ...), kind=kOutput, calls=%fused_computation.185 | convolution fusion | flops 3221504000 | bytes 16826368 | tf_op jit(solution)/shard_map/dot_general | solution.py:8
  (484 shorter events, 65.9 us)
Async XLA Ops:
  0.6 17.8 %copy-start.2 = (s32[16384,8]{0,1:T(8,128)S(1)}, s32[16384,8]{0,1:T(8,128)}, u32[]{:S(2)}) copy-start(s32[16384,8]{0,1:T(8,128)} %param.7) | copy-start | bytes 1572868
  0.6 18.7 %copy-start.3 = (f32[16384,8]{0,1:T(8,128)S(1)}, f32[16384,8]{0,1:T(8,128)}, u32[]{:S(2)}) copy-start(f32[16384,8]{0,1:T(8,128)} %param.8) | copy-start | bytes 1572868
  11.4 32.4 %all-to-all-start = ((f32[32,64,128]{2,1,0:T(8,128)}), f32[32,64,128]{2,1,0:T(8,128)S(1)}, u32[]{:S(2)}, u32[]{:S(2)}) async-start(f32[32,64,128]{2,1,0:T(8,128)} %bitcast.1), calls=%async_computation | async-start | bytes 2097152 | tf_op jit(solution)/shard_map/all_to_all | solution.py:39
  427.3 54.9 %copy-start.4 = (f32[16384,1]{0,1:T(1,128)S(1)}, f32[16384,1]{0,1:T(1,128)}, u32[]{:S(2)}) copy-start(f32[16384,1]{0,1:T(1,128)} %get-tuple-element.3) | copy-start | bytes 196612
  427.3 54.9 %copy-start.5 = (f32[16384,1]{0,1:T(1,128)S(1)}, f32[16384,1]{0,1:T(1,128)}, u32[]{:S(2)}) copy-start(f32[16384,1]{0,1:T(1,128)} %get-tuple-element.4) | copy-start | bytes 196612
  427.3 54.9 %copy-start.6 = (f32[16384,1]{0,1:T(1,128)S(1)}, f32[16384,1]{0,1:T(1,128)}, u32[]{:S(2)}) copy-start(f32[16384,1]{0,1:T(1,128)} %get-tuple-element.5) | copy-start | bytes 196612
  427.3 54.9 %copy-start.7 = (f32[16384,1]{0,1:T(1,128)S(1)}, f32[16384,1]{0,1:T(1,128)}, u32[]{:S(2)}) copy-start(f32[16384,1]{0,1:T(1,128)} %get-tuple-element.6) | copy-start | bytes 196612
  427.3 54.9 %copy-start.8 = (f32[16384,1]{0,1:T(1,128)S(1)}, f32[16384,1]{0,1:T(1,128)}, u32[]{:S(2)}) copy-start(f32[16384,1]{0,1:T(1,128)} %get-tuple-element.7) | copy-start | bytes 196612
  427.3 54.9 %copy-start.9 = (f32[16384,1]{0,1:T(1,128)S(1)}, f32[16384,1]{0,1:T(1,128)}, u32[]{:S(2)}) copy-start(f32[16384,1]{0,1:T(1,128)} %get-tuple-element.8) | copy-start | bytes 196612
  427.3 54.9 %copy-start.10 = (f32[16384,1]{0,1:T(1,128)S(1)}, f32[16384,1]{0,1:T(1,128)}, u32[]{:S(2)}) copy-start(f32[16384,1]{0,1:T(1,128)} %get-tuple-element.9) | copy-start | bytes 196612
  427.3 54.9 %copy-start.11 = (f32[16384,1]{0,1:T(1,128)S(1)}, f32[16384,1]{0,1:T(1,128)}, u32[]{:S(2)}) copy-start(f32[16384,1]{0,1:T(1,128)} %get-tuple-element.10) | copy-start | bytes 196612
  508.1 14.4 %copy-start.1 = (f32[16384,128]{1,0:T(8,128)}, f32[16384,128]{1,0:T(8,128)S(1)}, u32[]{:S(2)}) copy-start(f32[16384,128]{1,0:T(8,128)S(1)} %multiply_add_fusion) | copy-start | bytes 25165828
  522.5 2.1 collective-permute-start
  524.6 3.2 collective-permute-start.1
  527.8 3.2 collective-permute-start.2
  531.0 3.2 collective-permute-start.3
  534.2 4.8 collective-permute-start.4
  726.6 14.2 %copy-start = (f32[16384,128]{1,0:T(8,128)}, f32[16384,128]{1,0:T(8,128)S(1)}, u32[]{:S(2)}) copy-start(f32[16384,128]{1,0:T(8,128)S(1)} %fusion.13) | copy-start | bytes 25165828
  740.8 5.9 collective-permute-start.5
  746.7 3.2 collective-permute-start.6
  749.9 3.2 collective-permute-start.7
  753.1 3.2 collective-permute-start.8
  756.3 4.8 collective-permute-start.9
